TPU v7x, 512 devices: a whole 4x8x8 slice. The times are simulated.
512 devices in a mesh: rep: 4 (over x), node: 16 (over y, core), local: 8 (over z).
Axes of the slice: x: 4, y: 8, z: 8, core: 2. Of those that a mesh axis runs over, the one named last changes fastest.
Arguments:
- tokens: bfloat16 [8192, 4096], P(('rep', 'node', 'local')), may hold values from -6 to 6
- expert_ids: int32 [8192, 8], P(('rep', 'node', 'local')), may hold values from 0 to 127, all different within a row; in each aligned block of 16 rows (0 to 15, 16 to 31, ...) at most 2 rows name the same one
- route_weights: float32 [8192, 8], P(('rep', 'node', 'local')), may hold values from 0.1 to 1
- gate_weight: bfloat16 [128, 768, 4096], P(('node', 'local'), 'rep'), may hold values from -0.09375 to 0.09375
- up_weight: bfloat16 [128, 768, 4096], P(('node', 'local'), 'rep'), may hold values from -0.09375 to 0.09375
- down_weight: bfloat16 [128, 768, 4096], P(('node', 'local'), None, 'rep'), may hold values from -0.21875 to 0.21875
Outputs:
- mixed_rows: bfloat16 [8192, 4096], P(('rep', 'node', 'local'))
Inputs may be any that keep to these rules, and one draw needn't show every extreme that they name: `expert_ids`: each row names 8 different experts. Among the rows of one device (aligned blocks of 16 rows) no expert is named by more than 2 rows, and in some blocks some expert is named by exactly 2 rows.
All inputs are finite; a program needn't handle non-finite values.
Results may differ from a plain program's by a relative error of at most 0.0057.
Values may be sent and summed in bfloat16 or wider, within the bound.
A program may use at most 64 MiB of HBM per device.

v0:
```python
import jax
import jax.numpy as jnp
from jax import lax
from jax.sharding import PartitionSpec as P


def slot_table(expert_ids, expert_count, slot_cap):
    row_count, top_count = expert_ids.shape
    flat_ids = expert_ids.reshape(-1)
    same = flat_ids[:, None] == flat_ids[None, :]
    place = jnp.arange(row_count * top_count, dtype=jnp.int32)
    rank_of = jnp.sum((same & (place[None, :] < place[:, None])).astype(jnp.int32), axis=1)
    return (flat_ids * slot_cap + rank_of).reshape(row_count, top_count)


def route_slots(blocks):
    return lax.all_to_all(blocks, ("node", "local"), split_axis=1, concat_axis=1, tiled=True)


def on_device(tokens, expert_ids, route_weights, gate_weight, up_weight, down_weight):
    row_count, top_count = expert_ids.shape
    model_width = tokens.shape[1]
    node_count = lax.axis_size("node")
    plane_count = lax.axis_size("rep")
    expert_count = node_count * lax.axis_size("local")
    slot_cap = min(row_count, max(2, 2 * row_count * top_count // expert_count))
    slot_total = expert_count * slot_cap
    slot_of = slot_table(expert_ids, expert_count, slot_cap)
    slot_iota = jnp.arange(slot_total, dtype=jnp.int32)
    placed = jnp.any(slot_of[None, :, :] == slot_iota[:, None, None], axis=2).astype(jnp.bfloat16)
    outgoing = jnp.dot(placed, tokens, preferred_element_type=jnp.float32).astype(jnp.bfloat16)
    mixing = jnp.sum(
        jnp.where(slot_of[:, :, None] == slot_iota[None, None, :], route_weights[:, :, None], 0.0),
        axis=1,
    )
    arrived = route_slots(outgoing.reshape(1, expert_count, slot_cap, model_width))
    arrived = arrived.reshape(slot_total, model_width)
    gate_local = gate_weight[0]
    up_local = up_weight[0]
    down_local = down_weight[0]
    quarter_width = down_local.shape[1]
    feature_dims = (((1,), (1,)), ((), ()))
    shard_piece = lax.all_gather(arrived, "rep", axis=0, tiled=True)
    gate_part = lax.dot_general(
        shard_piece, gate_local, feature_dims, preferred_element_type=jnp.float32
    )
    up_part = lax.dot_general(
        shard_piece, up_local, feature_dims, preferred_element_type=jnp.float32
    )
    hidden_part = (jax.nn.silu(gate_part) * up_part).astype(jnp.bfloat16)
    expert_out = jnp.dot(
        lax.all_gather(hidden_part, "rep", axis=1, tiled=True),
        down_local,
        preferred_element_type=jnp.float32,
    ).astype(jnp.bfloat16)
    own_slots = lax.all_to_all(
        expert_out.reshape(plane_count, slot_total, quarter_width),
        "rep",
        split_axis=0,
        concat_axis=2,
        tiled=True,
    )
    returned = route_slots(own_slots.reshape(1, expert_count, slot_cap, model_width))
    back_rows = returned.reshape(slot_total, model_width).astype(jnp.float32)
    mixed_rows = jnp.dot(mixing, back_rows, precision=lax.Precision.HIGHEST)
    return mixed_rows.astype(jnp.bfloat16)


def solution(mesh):
    placed = (
        P(("rep", "node", "local"), None),
        P(("rep", "node", "local"), None),
        P(("rep", "node", "local"), None),
        P(("node", "local"), "rep", None),
        P(("node", "local"), "rep", None),
        P(("node", "local"), None, "rep"),
    )
    return jax.shard_map(
        on_device,
        mesh=mesh,
        in_specs=placed,
        out_specs=P(("rep", "node", "local"), None),
        check_vma=False,
    )
```

profile of v0, /device:TPU:1, one launch (start us, length us, event | category | flops | bytes accessed | tf_op | source)
XLA Modules:
  0.0 339.2 jit_solution(8202762404922500141)
XLA Ops:
  6.5 0.0 copy-start
  6.5 0.0 all-gather.3.cloned.1.call-start
  6.5 0.9 copy.20
  7.4 0.1 eq.20
  7.5 0.2 convert_reduce_fusion
  7.7 0.1 reduce_sum.21
  7.8 0.1 fusion.11
  7.9 3.0 convolution_convert_fusion
  10.9 4.4 %reshape.32 = bf16[1,128,2,4096]{3,2,1,0:T(2,128)(2,1)} reshape(bf16[256,4096]{1,0:T(8,128)(2,1)} %convolution_convert_fusion) | data formatting | bytes 4194304 | tf_op jit(solution)/shard_map/reshape | solution.py:36
  15.3 72.7 %all_to_all.25 = bf16[1,128,2,4096]{3,2,0,1:T(2,128)(2,1)} all-to-all(bf16[1,128,2,4096]{3,2,0,1:T(2,128)(2,1)} %bitcast.31), channel_id=1, replica_groups=mesh['rep'=4,'node'=16,'local'=8] {'node','local'}, dimensions={1} | all-to-all | bytes 4194304 | tf_op jit(solution)/shard_map/all_to_all | solution.py:17
  88.0 4.1 %reshape.33 = bf16[256,4096]{1,0:T(8,128)(2,1)} reshape(bf16[1,128,2,4096]{3,2,0,1:T(2,128)(2,1)} %all_to_all.25) | data formatting | bytes 4194304 | tf_op jit(solution)/shard_map/reshape | solution.py:37
  92.1 0.0 copy-start.3
  92.1 0.0 all-gather.3.cloned.1.call-update
  92.1 0.0 all-gather.5.cloned.1.call-start
  92.2 81.1 %all-gather.3.cloned.1.call-done = bf16[1024,4096]{1,0:T(8,128)(2,1)} async-done(((bf16[256,4096]{1,0:T(8,128)(2,1)}), bf16[1024,4096]{1,0:T(8,128)(2,1)}) %all-gather.3.cloned.1.call-update) | async-done | bytes 8388624 | tf_op jit(solution)/shard_map/all_gather | solution.py:43
  173.3 0.0 copy-done.3
  173.3 0.0 copy-start.2
  173.3 0.0 copy-start.4
  173.3 6.4 %fusion.3 = f32[1024,192]{0,1:T(8,128)S(1)} fusion(bf16[1024,4096]{1,0:T(8,128)(2,1)} %all-gather.3.cloned.1.call-done, bf16[1,192,4096]{2,1,0:T(8,128)(2,1)S(1)} %copy-done.3), kind=kOutput, calls=%fused_computation.6 | convolution fusion | flops 1610612736 | bytes 10747904 | tf_op jit(solution)/shard_map/dot_general | solution.py:44
  179.7 0.0 copy-done.2
  179.7 0.0 copy-done.4
  179.8 3.7 %fusion.8 = bf16[1024,192]{0,1:T(8,128)(2,1)} fusion(bf16[1024,4096]{1,0:T(8,128)(2,1)S(1)} %copy-done.2, bf16[1,192,4096]{2,1,0:T(8,128)(2,1)S(1)} %copy-done.4, f32[1024,192]{0,1:T(8,128)S(1)} %fusion.3), kind=kOutput, calls=%fused_computation.9 | convolution fusion | flops 1611792384 | bytes 11141120 | tf_op jit(solution)/shard_map/dot_general | solution.py:47
  183.4 0.0 all-gather.5.cloned.1.call-update
  183.5 33.0 %all-gather.5.cloned.1.call-done = bf16[1024,768]{0,1:T(8,128)(2,1)} async-done(((bf16[1024,192]{0,1:T(8,128)(2,1)}), bf16[1024,768]{0,1:T(8,128)(2,1)}) %all-gather.5.cloned.1.call-update) | async-done | bytes 1572880 | tf_op jit(solution)/shard_map/all_gather | solution.py:52
  216.5 0.0 copy-done
  216.5 3.2 convolution_convert_fusion.2
  219.7 27.8 %all_to_all.26 = bf16[4,256,1024]{2,1,0:T(8,128)(2,1)S(1)} all-to-all(bf16[4,256,1024]{2,1,0:T(8,128)(2,1)S(1)} %bitcast.33), channel_id=1, replica_groups=mesh['rep'=4,'node'=16,'local'=8] {'rep'}, dimensions={0} | all-to-all | bytes 4194304 | tf_op jit(solution)/shard_map/all_to_all | solution.py:56
  247.5 2.9 copy.24
  250.5 4.4 %reshape.35 = bf16[1,128,2,4096]{3,2,1,0:T(2,128)(2,1)} reshape(bf16[1,256,4,1024]{3,2,1,0:T(4,128)(2,1)} %copy.24) | data formatting | bytes 4194304 | tf_op jit(solution)/shard_map/reshape | solution.py:63
  254.8 0.0 copy-start.1
  254.8 16.4 %all-to-all-start.2 = ((bf16[1,128,2,4096]{3,2,0,1:T(2,128)(2,1)}), bf16[1,128,2,4096]{3,2,0,1:T(2,128)(2,1)}, u32[]{:S(2)}, u32[]{:S(2)}) async-start(bf16[1,128,2,4096]{3,2,0,1:T(2,128)(2,1)} %bitcast.30), calls=%async_computation.2 | async-start | bytes 4194304 | tf_op jit(solution)/shard_map/all_to_all | solution.py:17
  271.2 0.0 copy-done.1
  271.2 0.1 copy.22
  271.3 0.1 select_reduce_fusion
  271.4 53.6 %all-to-all-done.2 = bf16[1,128,2,4096]{3,2,0,1:T(2,128)(2,1)} async-done(((bf16[1,128,2,4096]{3,2,0,1:T(2,128)(2,1)}), bf16[1,128,2,4096]{3,2,0,1:T(2,128)(2,1)}, u32[]{:S(2)}, u32[]{:S(2)}) %all-to-all-start.2) | async-done | bytes 2097184 | tf_op jit(solution)/shard_map/all_to_all | solution.py:17
  325.0 4.1 %reshape.36 = bf16[256,4096]{1,0:T(8,128)(2,1)} reshape(bf16[1,128,2,4096]{3,2,0,1:T(2,128)(2,1)} %all-to-all-done.2) | data formatting | bytes 4194304 | tf_op jit(solution)/shard_map/reshape | solution.py:64
  329.1 3.2 convolution_convert_fusion.1
  (1 shorter events, 0.0 us)
Async XLA Ops:
  6.5 210.0 %copy-start = (bf16[1,768,1024]{2,1,0:T(8,128)(2,1)S(1)}, bf16[1,768,1024]{2,1,0:T(8,128)(2,1)}, u32[]{:S(2)}) copy-start(bf16[1,768,1024]{2,1,0:T(8,128)(2,1)} %param.11) | copy-start | bytes 4718596
  6.5 166.8 %all-gather.3.cloned.1.call-start = ((), (), s32[]{:S(2)}) async-start(), calls=%async_computation.3 | async-start | bytes 10485760 | tf_op jit(solution)/shard_map/all_gather | solution.py:43
  92.1 81.2 %copy-start.3 = (bf16[1,192,4096]{2,1,0:T(8,128)(2,1)S(1)}, bf16[1,192,4096]{2,1,0:T(8,128)(2,1)}, u32[]{:S(2)}) copy-start(bf16[1,192,4096]{2,1,0:T(8,128)(2,1)} %param.9) | copy-start | bytes 4718596
  92.1 124.4 %all-gather.5.cloned.1.call-start = ((), (), s32[]{:S(2)}) async-start(), calls=%async_computation.4 | async-start | bytes 1966080 | tf_op jit(solution)/shard_map/all_gather | solution.py:52
  173.3 6.4 %copy-start.2 = (bf16[1024,4096]{1,0:T(8,128)(2,1)S(1)}, bf16[1024,4096]{1,0:T(8,128)(2,1)}, u32[]{:S(2)}) copy-start(bf16[1024,4096]{1,0:T(8,128)(2,1)} %all-gather.3.cloned.1.call-done) | copy-start | bytes 25165828
  173.3 6.4 %copy-start.4 = (bf16[1,192,4096]{2,1,0:T(8,128)(2,1)S(1)}, bf16[1,192,4096]{2,1,0:T(8,128)(2,1)}, u32[]{:S(2)}) copy-start(bf16[1,192,4096]{2,1,0:T(8,128)(2,1)} %param.10) | copy-start | bytes 4718596
  254.8 16.4 %copy-start.1 = (f32[16,8]{0,1:T(8,128)S(1)}, f32[16,8]{0,1:T(8,128)}, u32[]{:S(2)}) copy-start(f32[16,8]{0,1:T(8,128)} %param.8) | copy-start | bytes 1540
  254.8 70.2 %all-to-all-start.2 = ((bf16[1,128,2,4096]{3,2,0,1:T(2,128)(2,1)}), bf16[1,128,2,4096]{3,2,0,1:T(2,128)(2,1)}, u32[]{:S(2)}, u32[]{:S(2)}) async-start(bf16[1,128,2,4096]{3,2,0,1:T(2,128)(2,1)} %bitcast.30), calls=%async_computation.2 | async-start | bytes 4194304 | tf_op jit(solution)/shard_map/all_to_all | solution.py:17
Sparse Core Ops, SparseCore 0:
  92.3 80.9 all-gather.2
  183.6 32.8 all-gather.4
where the time goes:
time: 340 us; the launch traced here: 339 us
  waiting for transfers between devices  168 us (49%)
  blocking collectives  100 us (29%)
  local copies, waits for them, and re-layouts  21.1 us (6%)
  matrix products  19.5 us (6%)
  starting transfers between devices  16.4 us (5%)
  between operations  13.5 us (4%)
    all_gather x1, waiting for transfers between devices, on_device(): shard_piece = lax.all_gather(arrived, 'rep', axis=0, tiled=True)  81.1 us
    all_to_all x1, blocking collectives, route_slots(): lax.all_to_all(blocks, ('node', 'local'), split_axis=1, concat_axis=1, ti...  72.7 us
    all_to_all x1, waiting for transfers between devices, route_slots(): lax.all_to_all(blocks, ('node', 'local'), split_axis=1, concat_axis=1, ti...  53.6 us
    all_gather x1, waiting for transfers between devices, on_device(): lax.all_gather(hidden_part, 'rep', axis=1, tiled=True)  33 us
    all_to_all x1, blocking collectives, on_device(): lax.all_to_all(expert_out.reshape(plane_count, slot_total, quarter_width)...  27.8 us
    all_to_all x1, starting transfers between devices, route_slots(): lax.all_to_all(blocks, ('node', 'local'), split_axis=1, concat_axis=1, ti...  16.4 us
  transfers between devices with their start and end apart: 3, of which 3 were waited for; matrix products, arithmetic and copies ran while one was open for 0% of the time, Pallas kernels for 0%

commit v1 on v0

--- a/solution.py
+++ b/solution.py
@@ -40,7 +40,16 @@
     down_local = down_weight[0]
     quarter_width = down_local.shape[1]
     feature_dims = (((1,), (1,)), ((), ()))
-    shard_piece = lax.all_gather(arrived, "rep", axis=0, tiled=True)
+    n_chips = lax.axis_size("rep")
+    x_new = sorted(((nth, (nth + 1) % n_chips) for nth in range(n_chips)))
+    x_now = arrived
+    line_up = [x_now]
+    for t in range(1, n_chips):
+        x_now = lax.ppermute(x_now, "rep", x_new)
+        line_up.insert(0, x_now)
+    out_arr = jnp.concatenate(line_up, 0)
+    e_now = lax.axis_index("rep")
+    shard_piece = jnp.roll(out_arr, (e_now + 1) * arrived.shape[0], 0)
     gate_part = lax.dot_general(
         shard_piece, gate_local, feature_dims, preferred_element_type=jnp.float32
     )

time: 340 us -> 408 us (1.20)
  waiting for transfers between devices: 168 us -> 220 us
  local copies, waits for them, and re-layouts: 21.1 us -> 33.3 us
  starting transfers between devices: 16.4 us -> 23.1 us
    ppermute x0 -> x3, waiting for transfers between devices: none -> 143 us  [on_device(): x_now = lax.ppermute(x_now, 'rep', x_new)]
    all_gather x1 -> x0, waiting for transfers between devices: 81.1 us -> none  [on_device(): shard_piece = lax.all_gather(arrived, 'rep', axis=0, tiled=True)]
    unnamed x12 -> x23, local copies, waits for them, and re-layouts: 0.97 us -> 13 us
    all_gather x1, waiting for transfers between devices: 33 us -> 23.1 us  [on_device(): lax.all_gather(hidden_part, 'rep', axis=1, tiled=True)]
    ppermute x0 -> x3, starting transfers between devices: none -> 6.93 us  [on_device(): x_now = lax.ppermute(x_now, 'rep', x_new)]
  transfers between devices with their start and end apart: 3 -> 5, of which waited for: 3 -> 5; matrix products, arithmetic and copies ran while one was open for 0% -> 0% of each run, Pallas kernels for 0% -> 0%
where the time goes in v1:
time: 408 us; the launch traced here: 407 us
  waiting for transfers between devices  220 us (54%)
  blocking collectives  100 us (25%)
  local copies, waits for them, and re-layouts  33.3 us (8%)
  starting transfers between devices  23.1 us (6%)
  matrix products  16 us (4%)
  between operations  13.6 us (3%)
    ppermute x3, waiting for transfers between devices, on_device(): x_now = lax.ppermute(x_now, 'rep', x_new)  143 us
    all_to_all x1, blocking collectives, route_slots(): lax.all_to_all(blocks, ('node', 'local'), split_axis=1, concat_axis=1, ti...  72.7 us
    all_to_all x1, waiting for transfers between devices, route_slots(): lax.all_to_all(blocks, ('node', 'local'), split_axis=1, concat_axis=1, ti...  53.6 us
    all_to_all x1, blocking collectives, on_device(): lax.all_to_all(expert_out.reshape(plane_count, slot_total, quarter_width)...  27.8 us
    all_gather x1, waiting for transfers between devices, on_device(): lax.all_gather(hidden_part, 'rep', axis=1, tiled=True)  23.1 us
    all_to_all x1, starting transfers between devices, route_slots(): lax.all_to_all(blocks, ('node', 'local'), split_axis=1, concat_axis=1, ti...  16.2 us
    unnamed x23, local copies, waits for them, and re-layouts  13 us
  transfers between devices with their start and end apart: 5, of which 5 were waited for; matrix products, arithmetic and copies ran while one was open for 0% of the time, Pallas kernels for 0%

profile of v1, /device:TPU:1, one launch (start us, length us, event | category | flops | bytes accessed | tf_op | source)
XLA Modules:
  0.0 406.6 jit_solution(17854523372832365783)
XLA Ops:
  6.5 0.0 copy-start
  6.5 0.0 all-gather.2.cloned.1.call-start
  6.5 0.9 copy.20
  7.4 0.1 eq.44
  7.5 0.2 convert_reduce_fusion
  7.7 0.1 reduce_sum.21
  7.8 0.1 fusion.7
  7.9 3.0 convolution_convert_fusion
  10.9 4.4 %reshape.32 = bf16[1,128,2,4096]{3,2,1,0:T(2,128)(2,1)} reshape(bf16[256,4096]{1,0:T(8,128)(2,1)} %convolution_convert_fusion) | data formatting | bytes 4194304 | tf_op jit(solution)/shard_map/reshape | solution.py:36
  15.3 72.7 %all_to_all.25 = bf16[1,128,2,4096]{3,2,0,1:T(2,128)(2,1)} all-to-all(bf16[1,128,2,4096]{3,2,0,1:T(2,128)(2,1)} %bitcast.27), channel_id=1, replica_groups=mesh['rep'=4,'node'=16,'local'=8] {'node','local'}, dimensions={1} | all-to-all | bytes 4194304 | tf_op jit(solution)/shard_map/all_to_all | solution.py:17
  88.0 4.1 %reshape.33 = bf16[256,4096]{1,0:T(8,128)(2,1)} reshape(bf16[1,128,2,4096]{3,2,0,1:T(2,128)(2,1)} %all_to_all.25) | data formatting | bytes 4194304 | tf_op jit(solution)/shard_map/reshape | solution.py:37
  92.1 3.1 collective-permute-start
  95.2 47.0 %collective-permute-done = bf16[256,4096]{1,0:T(8,128)(2,1)S(1)} collective-permute-done((bf16[256,4096]{1,0:T(8,128)(2,1)}, bf16[256,4096]{1,0:T(8,128)(2,1)S(1)}, u32[]{:S(2)}, u32[]{:S(2)}) %collective-permute-start) | collective-permute-done | bytes 2097184 | tf_op jit(solution)/shard_map/ppermute | solution.py:48
  142.2 0.0 copy-start.2
  142.2 1.3 copy-done.2
  143.5 1.9 collective-permute-start.1
  145.5 48.3 %collective-permute-done.1 = bf16[256,4096]{1,0:T(8,128)(2,1)} collective-permute-done((bf16[256,4096]{1,0:T(8,128)(2,1)S(1)}, bf16[256,4096]{1,0:T(8,128)(2,1)}, u32[]{:S(2)}, u32[]{:S(2)}) %collective-permute-start.1) | collective-permute-done | bytes 2097184 | tf_op jit(solution)/shard_map/ppermute | solution.py:48
  193.8 1.9 collective-permute-start.2
  195.7 47.6 %collective-permute-done.2 = bf16[256,4096]{1,0:T(8,128)(2,1)} collective-permute-done((bf16[256,4096]{1,0:T(8,128)(2,1)}, bf16[256,4096]{1,0:T(8,128)(2,1)}, u32[]{:S(2)}, u32[]{:S(2)}) %collective-permute-start.2) | collective-permute-done | bytes 2097184 | tf_op jit(solution)/shard_map/ppermute | solution.py:48
  243.3 1.8 constant_dynamic-update-slice_fusion.7
  245.1 0.0 copy-start.3
  245.1 1.9 constant_dynamic-update-slice_fusion.6
  247.1 0.3 copy-done.3
  247.4 0.0 copy-start.1
  247.4 0.1 constant_dynamic-update-slice_fusion.5
  247.5 1.4 copy-done.1
  248.9 0.1 constant_dynamic-update-slice_fusion.4
  249.1 1.8 constant_dynamic-update-slice_fusion.3
  250.9 1.8 constant_dynamic-update-slice_fusion.2
  252.7 0.1 constant_dynamic-update-slice_fusion.1
  252.8 0.0 copy-start.5
  252.9 0.1 constant_dynamic-update-slice_fusion
  253.0 1.3 copy-done.5
  254.3 0.0 copy-start.6
  254.3 2.9 fusion.2
  257.2 0.0 copy-done.6
  257.2 3.7 multiply_convert_fusion
  260.9 0.0 all-gather.2.cloned.1.call-update
  260.9 23.1 %all-gather.2.cloned.1.call-done = bf16[1024,768]{0,1:T(8,128)(2,1)} async-done(((bf16[1024,192]{0,1:T(8,128)(2,1)}), bf16[1024,768]{0,1:T(8,128)(2,1)}) %all-gather.2.cloned.1.call-update) | async-done | bytes 1572880 | tf_op jit(solution)/shard_map/all_gather | solution.py:61
  284.0 0.0 copy-done
  284.0 3.2 convolution_convert_fusion.2
  287.3 27.8 %all_to_all.26 = bf16[4,256,1024]{2,1,0:T(8,128)(2,1)S(1)} all-to-all(bf16[4,256,1024]{2,1,0:T(8,128)(2,1)S(1)} %bitcast.29), channel_id=1, replica_groups=mesh['rep'=4,'node'=16,'local'=8] {'rep'}, dimensions={0} | all-to-all | bytes 4194304 | tf_op jit(solution)/shard_map/all_to_all | solution.py:65
  315.0 3.0 copy.24
  318.0 4.4 %reshape.35 = bf16[1,128,2,4096]{3,2,1,0:T(2,128)(2,1)} reshape(bf16[1,256,4,1024]{3,2,1,0:T(4,128)(2,1)} %copy.24) | data formatting | bytes 4194304 | tf_op jit(solution)/shard_map/reshape | solution.py:72
  322.4 0.0 copy-start.4
  322.4 16.2 %all-to-all-start.2 = ((bf16[1,128,2,4096]{3,2,0,1:T(2,128)(2,1)}), bf16[1,128,2,4096]{3,2,0,1:T(2,128)(2,1)}, u32[]{:S(2)}, u32[]{:S(2)}) async-start(bf16[1,128,2,4096]{3,2,0,1:T(2,128)(2,1)} %bitcast.26), calls=%async_computation.2 | async-start | bytes 4194304 | tf_op jit(solution)/shard_map/all_to_all | solution.py:17
  338.6 0.0 copy-done.4
  338.6 0.1 copy.22
  338.7 0.1 select_reduce_fusion
  338.8 53.6 %all-to-all-done.2 = bf16[1,128,2,4096]{3,2,0,1:T(2,128)(2,1)} async-done(((bf16[1,128,2,4096]{3,2,0,1:T(2,128)(2,1)}), bf16[1,128,2,4096]{3,2,0,1:T(2,128)(2,1)}, u32[]{:S(2)}, u32[]{:S(2)}) %all-to-all-start.2) | async-done | bytes 2097184 | tf_op jit(solution)/shard_map/all_to_all | solution.py:17
  392.4 4.1 %reshape.36 = bf16[256,4096]{1,0:T(8,128)(2,1)} reshape(bf16[1,128,2,4096]{3,2,0,1:T(2,128)(2,1)} %all-to-all-done.2) | data formatting | bytes 4194304 | tf_op jit(solution)/shard_map/reshape | solution.py:73
  396.5 3.2 convolution_convert_fusion.1
  (1 shorter events, 0.0 us)
Async XLA Ops:
  6.5 277.5 %copy-start = (bf16[1,768,1024]{2,1,0:T(8,128)(2,1)S(1)}, bf16[1,768,1024]{2,1,0:T(8,128)(2,1)}, u32[]{:S(2)}) copy-start(bf16[1,768,1024]{2,1,0:T(8,128)(2,1)} %param.11) | copy-start | bytes 4718596
  6.5 277.5 %all-gather.2.cloned.1.call-start = ((), (), s32[]{:S(2)}) async-start(), calls=%async_computation.3 | async-start | bytes 1966080 | tf_op jit(solution)/shard_map/all_gather | solution.py:61
  92.1 50.1 %collective-permute-start = (bf16[256,4096]{1,0:T(8,128)(2,1)}, bf16[256,4096]{1,0:T(8,128)(2,1)S(1)}, u32[]{:S(2)}, u32[]{:S(2)}) collective-permute-start(bf16[256,4096]{1,0:T(8,128)(2,1)} %reshape.33), channel_id=1, source_target_pairs={{0,128},{128,256},{256,384},{384,0},{1,129},{129,257},{257,385},{3... | collective-permute-start | bytes 6291464 | tf_op jit(solution)/shard_map/ppermute | solution.py:48
  142.2 1.3 copy-start.2
  143.5 50.2 %collective-permute-start.1 = (bf16[256,4096]{1,0:T(8,128)(2,1)S(1)}, bf16[256,4096]{1,0:T(8,128)(2,1)}, u32[]{:S(2)}, u32[]{:S(2)}) collective-permute-start(bf16[256,4096]{1,0:T(8,128)(2,1)S(1)} %collective-permute-done), channel_id=1, source_target_pairs={{0,128},{128,256},{256,384},{384,0},{1,129},{129,257},{257,385},{3... | collective-permute-start | bytes 6291464 | tf_op jit(solution)/shard_map/ppermute | solution.py:48
  193.8 49.5 %collective-permute-start.2 = (bf16[256,4096]{1,0:T(8,128)(2,1)}, bf16[256,4096]{1,0:T(8,128)(2,1)}, u32[]{:S(2)}, u32[]{:S(2)}) collective-permute-start(bf16[256,4096]{1,0:T(8,128)(2,1)} %collective-permute-done.1), channel_id=1, source_target_pairs={{0,128},{128,256},{256,384},{384,0},{1,129},{129,257},{257,385},{3... | collective-permute-start | bytes 6291464 | tf_op jit(solution)/shard_map/ppermute | solution.py:48
  245.1 2.2 copy-start.3
  247.4 1.6 copy-start.1
  252.8 1.4 copy-start.5
  254.3 2.9 copy-start.6
  322.4 16.2 %copy-start.4 = (f32[16,8]{0,1:T(8,128)S(1)}, f32[16,8]{0,1:T(8,128)}, u32[]{:S(2)}) copy-start(f32[16,8]{0,1:T(8,128)} %param.8) | copy-start | bytes 1540
  322.4 70.0 %all-to-all-start.2 = ((bf16[1,128,2,4096]{3,2,0,1:T(2,128)(2,1)}), bf16[1,128,2,4096]{3,2,0,1:T(2,128)(2,1)}, u32[]{:S(2)}, u32[]{:S(2)}) async-start(bf16[1,128,2,4096]{3,2,0,1:T(2,128)(2,1)} %bitcast.26), calls=%async_computation.2 | async-start | bytes 4194304 | tf_op jit(solution)/shard_map/all_to_all | solution.py:17
Sparse Core Ops, SparseCore 0:
  261.1 22.9 all-gather.1
